TPU v7x, 32 devices: a whole 2x2x4 slice. The times are simulated.
32 devices in a mesh: dp: 4 (over y, x), mp: 8 (over z, core).
Axes of the slice: x: 2, y: 2, z: 4, core: 2. Of those that a mesh axis runs over, the one named last changes fastest.
Arguments:
- tokens: bfloat16 [1024, 8192], P('dp', 'mp'), may hold values from -6 to 6
- base_weight: bfloat16 [24576, 8192], P('mp'), may hold values from -0.0625 to 0.0625
- block_values: bfloat16 [256, 128, 128], P('mp'), may hold values from -0.0625 to 0.0625
- block_ids: int32 [2, 256], P(None, 'mp'), may hold values from -1 to 63, as said below
- lowrank_model: float32 [8192, 256], P('mp'), may hold values from -6 to 6
- lowrank_hidden: float32 [24576, 256], P('mp'), may hold values from -6 to 6
- output_cotangent: bfloat16 [1024, 24576], P('dp', 'mp'), may hold values from -6 to 6
Outputs:
- projection_output: bfloat16 [1024, 24576], P('dp', 'mp')
- input_cotangent: bfloat16 [1024, 8192], P('dp', 'mp')
- block_grads: float32 [256, 128, 128], P(('mp', 'dp'))
- updated_model: float32 [8192, 256], P('mp')
- updated_hidden: float32 [24576, 256], P('mp')
Inputs may be any that keep to these rules, and one draw needn't show every extreme that they name: `block_ids`: slots 32 * m to 32 * (m + 1) - 1 belong to index m of mp. A live slot has row 0 in 0 to 23 and row 1 in 0 to 63; the live slots of one index come first and name distinct blocks; the remaining slots hold -1 in both rows. Every index has 8 or more live slots, and some index has all 32.
All inputs are finite; a program needn't handle non-finite values.
Results may differ from a plain program's by a relative error of at most 0.0065.
Values may be sent and summed in bfloat16 or wider, within the bound.
A program may use at most 384 MiB of HBM per device.

v0:
```python
import math

import jax
import jax.numpy as jnp
from jax import lax
from jax.sharding import PartitionSpec as P


def partner_2(value, axis, distance):
    return lax.ppermute(value, axis, [(i, i ^ 1 << distance) for i in range(lax.axis_size(axis))])


def shards(
    tokens, base_weight, block_values, block_ids, lowrank_model, lowrank_hidden, output_cotangent
):
    tok_rows = tokens.shape[0]
    mp_size = lax.axis_size("mp")
    dp_size = lax.axis_size("dp")
    total_tokens = tok_rows * dp_size
    f_local = base_weight.shape[0]
    feature_width = base_weight.shape[1]
    hidden_total = f_local * mp_size
    nb_local = block_values.shape[0]
    block_size = block_values.shape[1]
    adapter_factor_rank = lowrank_model.shape[1]
    col_blocks = feature_width // block_size
    row_blocks = f_local // block_size
    adapter_scale = 0.5 / math.sqrt(adapter_factor_rank * feature_width)
    row_ids = block_ids[0]
    col_ids = block_ids[1]
    live_slots = row_ids >= 0
    flat_index = jnp.where(live_slots, row_ids * col_blocks + col_ids, -1)
    placer = (
        flat_index[:, None] == jnp.arange(row_blocks * col_blocks, dtype=jnp.int32)[None, :]
    ).astype(jnp.bfloat16)
    dense_blocks = lax.dot_general(
        placer,
        block_values.reshape(nb_local, block_size * block_size),
        (((0,), (0,)), ((), ())),
        preferred_element_type=jnp.float32,
    )
    dense_blocks = (
        dense_blocks.reshape(row_blocks, col_blocks, block_size, block_size)
        .transpose(0, 2, 1, 3)
        .reshape(f_local, feature_width)
    )
    effective = (base_weight.astype(jnp.float32) + dense_blocks).astype(jnp.bfloat16)
    gathered = lax.all_gather(tokens, "mp", axis=1, tiled=True)
    model_half = lowrank_model.astype(jnp.bfloat16)
    hidden_half = lowrank_hidden.astype(jnp.bfloat16)
    v_partial = jnp.dot(output_cotangent, hidden_half, preferred_element_type=jnp.float32)
    model_rows = lax.all_gather(model_half, "mp", axis=0, tiled=True)
    u_summed = jnp.dot(gathered, model_rows, preferred_element_type=jnp.float32)
    v_summed = lax.psum(v_partial, "mp")
    left_factor_shard = u_summed.astype(jnp.bfloat16)
    right_factor_shard = v_summed.astype(jnp.bfloat16)
    base_projection_output = lax.dot_general(
        gathered, effective, (((1,), (1,)), ((), ())), preferred_element_type=jnp.float32
    )
    lowrank_output = lax.dot_general(
        left_factor_shard, hidden_half, (((1,), (1,)), ((), ())), preferred_element_type=jnp.float32
    )
    projection_output = (base_projection_output + adapter_scale * lowrank_output).astype(
        jnp.bfloat16
    )
    backward_lowrank_term = lax.dot_general(
        right_factor_shard, model_half, (((1,), (1,)), ((), ())), preferred_element_type=jnp.float32
    )
    backward_base_term = lax.psum_scatter(
        lax.dot_general(
            effective,
            output_cotangent,
            (((0,), (1,)), ((), ())),
            preferred_element_type=jnp.float32,
        ),
        "mp",
        scatter_dimension=0,
        tiled=True,
    ).T
    input_cotangent = (backward_base_term + adapter_scale * backward_lowrank_term).astype(
        jnp.bfloat16
    )
    right_factor_gradient_part = adapter_scale * lax.dot_general(
        output_cotangent,
        left_factor_shard,
        (((0,), (0,)), ((), ())),
        preferred_element_type=jnp.float32,
    )
    left_factor_gradient_part = adapter_scale * lax.dot_general(
        tokens, right_factor_shard, (((0,), (0,)), ((), ())), preferred_element_type=jnp.float32
    )
    hidden_side_gradient, model_side_gradient = (
        lax.psum(right_factor_gradient_part.astype(jnp.bfloat16), "dp").astype(jnp.float32),
        lax.psum(left_factor_gradient_part.astype(jnp.bfloat16), "dp").astype(jnp.float32),
    )
    safe_rows = jnp.maximum(row_ids, 0)
    safe_cols = jnp.maximum(col_ids, 0)
    grad_sel = jnp.take(
        output_cotangent.reshape(tok_rows, row_blocks, block_size), safe_rows, axis=1
    )
    token_sel = jnp.take(gathered.reshape(tok_rows, col_blocks, block_size), safe_cols, axis=1)
    block_part = jnp.einsum("tbi,tbj->bij", grad_sel, token_sel, preferred_element_type=jnp.float32)
    block_part = (
        block_part * (live_slots.astype(jnp.float32) / math.sqrt(total_tokens))[:, None, None]
    )
    block_grads = lax.psum_scatter(block_part, "dp", scatter_dimension=0, tiled=True)
    model_step = (
        lowrank_model
        - math.sqrt(adapter_factor_rank * feature_width / (total_tokens * hidden_total))
        * model_side_gradient
    )
    moved_hidden = (
        lowrank_hidden - math.sqrt(adapter_factor_rank / total_tokens) * hidden_side_gradient
    )
    gram_local = lax.dot_general(
        moved_hidden, moved_hidden, (((0,), (0,)), ((), ())), precision=lax.Precision.HIGHEST
    )
    lower_factor = jnp.linalg.cholesky(gram_local)
    levels = mp_size.bit_length() - 1
    for bit_index in range(levels):
        partner = partner_2(lower_factor.astype(jnp.bfloat16), "mp", bit_index).astype(
            lower_factor.dtype
        )
        own_gram = jnp.dot(lower_factor, lower_factor.T, precision=lax.Precision.HIGHEST)
        partner_gram = jnp.dot(partner, partner.T, precision=lax.Precision.HIGHEST)
        lower_factor = jnp.linalg.cholesky(own_gram + partner_gram)
    solved = lax.linalg.triangular_solve(
        lower_factor, moved_hidden, left_side=False, lower=True, transpose_a=True
    )
    updated_hidden = math.sqrt(hidden_total) * solved
    updated_model = jnp.dot(model_step, lower_factor, precision=lax.Precision.HIGHEST) / math.sqrt(
        hidden_total
    )
    return (projection_output, input_cotangent, block_grads, updated_model, updated_hidden)


def solution(mesh):
    in_specs = (
        P("dp", "mp"),
        P("mp", None),
        P("mp", None, None),
        P(None, "mp"),
        P("mp", None),
        P("mp", None),
        P("dp", "mp"),
    )
    out_specs = (
        P("dp", "mp"),
        P("dp", "mp"),
        P(("mp", "dp"), None, None),
        P("mp", None),
        P("mp", None),
    )
    return jax.shard_map(shards, mesh=mesh, in_specs=in_specs, out_specs=out_specs, check_vma=False)
```

profile of v0, /device:TPU:0, one launch (start us, length us, event | category | flops | bytes accessed | tf_op | source)
XLA Modules:
  0.0 534.9 jit_solution(5461947114065312162)
XLA Ops:
  14.3 39.6 %all-reduce.6 = bf16[256,256]{1,0:T(8,128)(2,1)S(1)} all-reduce(f32[256,256]{1,0:T(8,128)S(1)} %fusion.29), channel_id=1, replica_groups=mesh['dp'=4,'mp'=8] {'mp'}, use_global_device_ids=true, to_apply=%region_1.2 | all-reduce | flops 65536 | bytes 393216 | tf_op jit(solution)/shard_map/psum | solution.py:54
  56.1 37.0 %fusion.23 = f32[24,64,128,128]{3,1,2,0:T(8,128)} fusion(s32[24,64]{1,0:T(8,128)S(1)} %multiply_add_fusion, s32[32]{0:T(128)S(1)} %get-tuple-element.61, bf16[4,8,128,128]{3,2,1,0:T(8,128)(2,1)} %bitcast.154), kind=kOutput, calls=%fused_computation.40 | convolution fusion | flops 1610661888 | bytes 101718144 | tf_op jit(solution)/shard_map/dot_general | solution.py:36
  93.1 19.2 %all-gather.5.cloned.1.call-done = bf16[8192,256]{1,0:T(8,128)(2,1)} async-done(((bf16[1024,256]{1,0:T(8,128)(2,1)}), bf16[8192,256]{1,0:T(8,128)(2,1)}) %all-gather.5.cloned.1.call-update) | async-done | bytes 4194320 | tf_op jit(solution)/shard_map/all_gather | solution.py:52
  112.3 4.9 convolution_convert_fusion
  119.7 56.7 %fusion.106 = f32[8192,256]{1,0:T(8,128)} fusion(bf16[256,3072]{1,0:T(8,128)(2,1)} %param.14, f32[384,8,64,128]{3,2,1,0:T(8,128)} %bitcast.42, bf16[3072,8192]{1,0:T(8,128)(2,1)} %param.9), kind=kOutput, calls=%fused_computation.165 | convolution fusion | flops 12960399360 | bytes 160956416 | tf_op jit(solution)/shard_map/dot_general | solution.py:70
  181.7 3.6 gather_fusion
  185.3 91.2 %convolution_bitcast_fusion = f32[256,3072]{0,1:T(8,128)} fusion(bf16[256,8192]{0,1:T(8,128)(2,1)} %all-gather.3.cloned.1.call-done, f32[384,8,64,128]{3,2,1,0:T(8,128)} %bitcast.42, bf16[3072,8192]{1,0:T(8,128)(2,1)} %param.9), kind=kOutput, calls=%fused_computation.6 | convolution fusion | flops 12960399360 | bytes 158334976 | tf_op jit(solution)/shard_map/dot_general | solution.py:57
  276.4 3.7 fusion.2
  282.7 6.8 %copy.53 = bf16[256,64,128]{2,0,1:T(8,128)(2,1)} copy(bf16[256,64,128]{0,2,1:T(8,128)(2,1)} %bitcast.152) | data formatting | bytes 8388608 | tf_op jit(solution)/shard_map/reshape | solution.py:101
  289.5 4.5 gather_fusion.1
  293.9 3.9 fusion.14
  300.6 5.1 fusion.110
  308.2 11.7 %cholesky.214 = f32[128,128]{1,0:T(8,128)S(1)} custom-call(f32[128,128]{1,0:T(8,128)S(1)} %cholesky.346), custom_call_target="Cholesky" | custom-call | tf_op jit(solution)/shard_map/jit(cholesky)/cholesky | solution.py:118
  320.0 10.0 %custom-call.15 = f32[1,128,128]{1,2,0:T(8,128)S(1)} custom-call(f32[1,128,128]{2,1,0:T(8,128)S(1)} %get-tuple-element.56), custom_call_target="InvertDiagBlocksLowerTriangular" | custom-call | tf_op jit(solution)/shard_map/jit(cholesky)/cholesky | solution.py:118
  332.1 11.7 %cholesky.231 = f32[128,128]{1,0:T(8,128)S(1)} custom-call(f32[128,128]{1,0:T(8,128)S(1)} %convolution_subtract_fusion.1), custom_call_target="Cholesky" | custom-call | tf_op jit(solution)/shard_map/jit(cholesky)/cholesky | solution.py:118
  350.1 11.7 %cholesky.248 = f32[128,128]{1,0:T(8,128)S(1)} custom-call(f32[128,128]{1,0:T(8,128)S(1)} %cholesky.349), custom_call_target="Cholesky" | custom-call | tf_op jit(solution)/shard_map/jit(cholesky)/cholesky | solution.py:126
  361.9 9.8 %custom-call.16 = f32[1,128,128]{1,2,0:T(8,128)S(1)} custom-call(f32[1,128,128]{2,1,0:T(8,128)S(1)} %get-tuple-element.52), custom_call_target="InvertDiagBlocksLowerTriangular" | custom-call | tf_op jit(solution)/shard_map/jit(cholesky)/cholesky | solution.py:126
  373.8 11.9 %cholesky.265 = f32[128,128]{1,0:T(8,128)S(1)} custom-call(f32[128,128]{1,0:T(8,128)S(1)} %slice_subtract_fusion.2), custom_call_target="Cholesky" | custom-call | tf_op jit(solution)/shard_map/jit(cholesky)/cholesky | solution.py:126
  389.5 4.7 collective-permute-done.1
  397.0 11.7 %cholesky.282 = f32[128,128]{1,0:T(8,128)S(1)} custom-call(f32[128,128]{1,0:T(8,128)S(1)} %cholesky.352), custom_call_target="Cholesky" | custom-call | tf_op jit(solution)/shard_map/jit(cholesky)/cholesky | solution.py:126
  408.8 9.8 %custom-call.17 = f32[1,128,128]{1,2,0:T(8,128)S(1)} custom-call(f32[1,128,128]{2,1,0:T(8,128)S(1)} %get-tuple-element.48), custom_call_target="InvertDiagBlocksLowerTriangular" | custom-call | tf_op jit(solution)/shard_map/jit(cholesky)/cholesky | solution.py:126
  420.7 12.1 %cholesky.299 = f32[128,128]{1,0:T(8,128)S(1)} custom-call(f32[128,128]{1,0:T(8,128)S(1)} %slice_subtract_fusion.1), custom_call_target="Cholesky" | custom-call | tf_op jit(solution)/shard_map/jit(cholesky)/cholesky | solution.py:126
  437.4 6.4 %collective-permute-done.2 = bf16[256,256]{1,0:T(8,128)(2,1)S(1)} collective-permute-done((bf16[256,256]{1,0:T(8,128)(2,1)S(1)}, bf16[256,256]{1,0:T(8,128)(2,1)S(1)}, u32[]{:S(2)}, u32[]{:S(2)}) %collective-permute-start.2) | collective-permute-done | bytes 131104 | tf_op jit(solution)/shard_map/ppermute | solution.py:10
  446.6 11.7 %cholesky.316 = f32[128,128]{1,0:T(8,128)S(1)} custom-call(f32[128,128]{1,0:T(8,128)S(1)} %cholesky.355), custom_call_target="Cholesky" | custom-call | tf_op jit(solution)/shard_map/jit(cholesky)/cholesky | solution.py:126
  458.4 9.8 %custom-call.18 = f32[1,128,128]{1,2,0:T(8,128)S(1)} custom-call(f32[1,128,128]{2,1,0:T(8,128)S(1)} %get-tuple-element.44), custom_call_target="InvertDiagBlocksLowerTriangular" | custom-call | tf_op jit(solution)/shard_map/jit(cholesky)/cholesky | solution.py:126
  470.3 11.9 %cholesky.333 = f32[128,128]{1,0:T(8,128)S(1)} custom-call(f32[128,128]{1,0:T(8,128)S(1)} %slice_subtract_fusion), custom_call_target="Cholesky" | custom-call | tf_op jit(solution)/shard_map/jit(cholesky)/cholesky | solution.py:126
  485.6 6.8 %while.1 = (s32[]{:T(128)}, f32[256,256]{1,0:T(8,128)}, s32[2,2]{1,0:T(2,128)S(1)}, f32[2,128,128]{2,1,0:T(8,128)}, s32[]{:T(128)}) while((s32[]{:T(128)}, f32[256,256]{1,0:T(8,128)}, s32[2,2]{1,0:T(2,128)S(1)}, f32[2,128,128]{2,1,0:T(8,128)}, s32[]{:T(128)}) %tuple.44), condition=%wide.while_cond, body=%wide.while_body.sunk | while | flops 2 | bytes 132205 | solution.py:127
  486.2 2.8 bitcast_dynamic-update-slice_fusion.2
  489.6 2.8 bitcast_dynamic-update-slice_fusion.2
  492.4 20.5 %custom-call.11 = f32[2,128,128]{1,2,0:T(8,128)S(1)} custom-call(f32[2,128,128]{2,1,0:T(8,128)} %get-tuple-element.13), custom_call_target="InvertDiagBlocksLowerTriangular" | custom-call | tf_op jit(solution)/shard_map/triangular_solve | solution.py:127
  514.5 3.5 convolution_subtract_fusion
  522.2 3.4 convolution_multiply_fusion.4
  (122 shorter events, 61.4 us)
Async XLA Ops:
  7.2 4.5 copy-start
  7.2 85.9 %all-gather.3.cloned.1.call-start = ((), (), s32[]{:S(2)}) async-start(), calls=%async_computation.2 | async-start | bytes 4718592 | tf_op jit(solution)/shard_map/all_gather | solution.py:48
  9.4 102.9 %all-gather.5.cloned.1.call-start = ((), (), s32[]{:S(2)}) async-start(), calls=%async_computation.3 | async-start | bytes 4718592 | tf_op jit(solution)/shard_map/all_gather | solution.py:52
  11.6 2.1 copy-start.10
  11.6 286.3 %all-reduce.5.cloned.1.call-start = ((), (), s32[]{:S(2)}) async-start(), calls=%async_computation.6 | async-start | bytes 4194304 | tf_op jit(solution)/shard_map/psum | solution.py:94
  53.9 39.2 %copy-start.4 = (bf16[256,256]{1,0:T(8,128)(2,1)}, bf16[256,256]{1,0:T(8,128)(2,1)S(1)}, u32[]{:S(2)}) copy-start(bf16[256,256]{1,0:T(8,128)(2,1)S(1)} %all-reduce.6) | copy-start | bytes 393220
  112.3 4.9 copy-start.1
  119.2 406.5 %reduce-scatter.3.cloned.1.call-start = ((), (), s32[]{:S(2)}) async-start(), calls=%async_computation.4 | async-start | bytes 9437184 | tf_op jit(solution)/shard_map/reduce_scatter | solution.py:69
  176.4 5.3 copy-start.12
  176.4 5.3 copy-start.13
  176.4 351.8 %reduce-scatter.5.cloned.1.call-start = ((), (), s32[]{:S(2)}) async-start(), calls=%async_computation.5 | async-start | bytes 2621440 | tf_op jit(solution)/shard_map/reduce_scatter | solution.py:106
  179.1 6.2 %copy-start.11 = (s32[2,32]{1,0:T(2,128)S(1)}, s32[2,32]{1,0:T(2,128)}, u32[]{:S(2)}) copy-start(s32[2,32]{1,0:T(2,128)} %param.11) | copy-start | bytes 772
  289.5 4.5 copy-start.3
  307.5 0.7 copy-start.7
  345.9 1.5 collective-permute-start
  349.4 0.7 copy-start.8
  388.4 5.8 %collective-permute-start.1 = (bf16[256,256]{1,0:T(8,128)(2,1)S(1)}, bf16[256,256]{1,0:T(8,128)(2,1)S(1)}, u32[]{:S(2)}, u32[]{:S(2)}) collective-permute-start(bf16[256,256]{1,0:T(8,128)(2,1)S(1)} %fusion.46), channel_id=1, source_target_pairs={{0,2},{1,3},{2,0},{3,1},{4,6},{5,7},{6,4},{7,5},{8,10},{9,11},{10,... | collective-permute-start | bytes 393224 | tf_op jit(solution)/shard_map/ppermute | solution.py:10
  396.3 0.7 copy-start.9
  435.5 8.3 %collective-permute-start.2 = (bf16[256,256]{1,0:T(8,128)(2,1)S(1)}, bf16[256,256]{1,0:T(8,128)(2,1)S(1)}, u32[]{:S(2)}, u32[]{:S(2)}) collective-permute-start(bf16[256,256]{1,0:T(8,128)(2,1)S(1)} %fusion.43), channel_id=1, source_target_pairs={{0,4},{1,5},{2,6},{3,7},{4,0},{5,1},{6,2},{7,3},{8,12},{9,13},{10,... | collective-permute-start | bytes 393224 | tf_op jit(solution)/shard_map/ppermute | solution.py:10
  445.9 0.7 copy-start.6
  519.8 5.8 %copy-start.5 = (bf16[256,256]{1,0:T(8,128)(2,1)S(1)}, bf16[256,256]{1,0:T(8,128)(2,1)}, u32[]{:S(2)}) copy-start(bf16[256,256]{1,0:T(8,128)(2,1)} %copy-done.4) | copy-start | bytes 393220
  522.2 3.4 copy-start.2
Sparse Core Ops, SparseCore 0:
  10.2 53.7 all-gather.2
  66.2 46.1 all-gather.4
  119.3 68.2 all-reduce.4
  189.8 89.5 reduce-scatter.2
  298.0 34.5 reduce-scatter.4
where the time goes:
time: 541 us; the launch traced here: 535 us
  matrix products  231 us (43%)
  other arithmetic  169 us (31%)
  local copies, waits for them, and re-layouts  41.3 us (8%)
  blocking collectives  39.6 us (7%)
  waiting for transfers between devices  31 us (6%)
  between operations  19.6 us (4%)
    another operation x21, other arithmetic, shards(): lower_factor = jnp.linalg.cholesky(own_gram + partner_gram)  104 us
    dot_general x1, matrix products, shards(): lax.dot_general(gathered, effective, (((1,), (1,)), ((), ())), preferred_...  91.2 us
    dot_general x1, matrix products, shards(): lax.dot_general(effective, output_cotangent, (((0,), (1,)), ((), ())), pr...  56.7 us
    psum x1, blocking collectives, shards(): v_summed = lax.psum(v_partial, 'mp')  39.6 us
    dot_general x1, matrix products, shards(): lax.dot_general(placer, block_values.reshape(nb_local, block_size * block...  37 us
    another operation x6, other arithmetic, shards(): lower_factor = jnp.linalg.cholesky(gram_local)  34.1 us
    another operation x3, other arithmetic, shards(): lax.linalg.triangular_solve(lower_factor, moved_hidden, left_side=False,...  21.2 us
    all_gather x1, waiting for transfers between devices, shards(): model_rows = lax.all_gather(model_half, 'mp', axis=0, tiled=True)  19.2 us
  transfers between devices with their start and end apart: 8, of which 4 were waited for; matrix products, arithmetic and copies ran while one was open for 80% of the time, Pallas kernels for 0%

commit v1 on v0

v1 whole, which is shorter than its diff:
```python
import functools
import math

import jax
import jax.numpy as jnp
from jax import lax
from jax.experimental import pallas as pl
from jax.experimental.pallas import tpu as pltpu
from jax.sharding import PartitionSpec as P

HIGHEST = lax.Precision.HIGHEST


def largest_divisor(total, step, most):
    return max(c for c in range(step, most + 1, step) if total % c == 0)


def dense_kernel(
    lora_scale,
    grad_scale,
    tile,
    chunk,
    ids_ref,
    tok_ref,
    cot_ref,
    hid_ref,
    u_ref,
    vals_ref,
    base_ref,
    out_ref,
    back_ref,
    grads_ref,
    buf,
    acc_out,
    acc_back,
    sem,
):
    hidden, width = base_ref.shape
    slots, side = vals_ref.shape[0], vals_ref.shape[1]
    parts, _, part_width = back_ref.shape
    tiles = hidden // tile
    per_tile = tile // side

    def fetch(step, slot):
        rows = pl.ds(pl.multiple_of(step * tile, tile), tile)
        return pltpu.make_async_copy(base_ref.at[rows], buf.at[slot], sem.at[slot])

    fetch(0, 0).start()
    grads_ref[...] = jnp.zeros_like(grads_ref)

    @pl.loop(0, tiles)
    def _(step):
        slot = lax.rem(step, 2)

        @pl.when(step + 1 < tiles)
        def _():
            fetch(step + 1, 1 - slot).start()

        fetch(step, slot).wait()

        @pl.loop(0, slots)
        def _(s):
            row = ids_ref[0, s]

            @pl.when((row >= step * per_tile) & (row < (step + 1) * per_tile))
            def _():
                cols = pl.ds(pl.multiple_of(ids_ref[1, s] * side, side), side)
                inner = pl.ds(pl.multiple_of((row - step * per_tile) * side, side), side)
                outer = pl.ds(pl.multiple_of(row * side, side), side)
                old = buf[slot, inner, cols].astype(jnp.float32)
                buf[slot, inner, cols] = (old + vals_ref[s].astype(jnp.float32)).astype(buf.dtype)
                block = lax.dot_general(
                    cot_ref[:, outer],
                    tok_ref[:, cols],
                    (((0,), (0,)), ((), ())),
                    preferred_element_type=jnp.float32,
                )
                grads_ref[s] = (block * grad_scale).astype(grads_ref.dtype)

        rows = pl.ds(pl.multiple_of(step * tile, tile), tile)
        acc_out[...] = lora_scale * lax.dot_general(
            u_ref[...],
            hid_ref[rows, :],
            (((1,), (1,)), ((), ())),
            preferred_element_type=jnp.float32,
        )

        @pl.loop(0, width // chunk)
        def _(c):
            cols = pl.ds(pl.multiple_of(c * chunk, chunk), chunk)
            weights = buf[slot, :, cols]
            acc_out[...] += lax.dot_general(
                tok_ref[:, cols],
                weights,
                (((1,), (1,)), ((), ())),
                preferred_element_type=jnp.float32,
            )
            term = jnp.dot(cot_ref[:, rows], weights, preferred_element_type=jnp.float32)

            @pl.when(step == 0)
            def _():
                acc_back[:, cols] = term

            @pl.when(step > 0)
            def _():
                acc_back[:, cols] += term

        out_ref[:, rows] = acc_out[...].astype(out_ref.dtype)

    for part in range(parts):
        back_ref[part] = acc_back[:, part * part_width : (part + 1) * part_width].astype(
            back_ref.dtype
        )


def dense(ids, gathered, cotangent, hidden_half, u_half, values, base, parts, lora_scale, grad_scale):
    rows, width = gathered.shape
    hidden = base.shape[0]
    tile = largest_divisor(hidden, values.shape[1], 512)
    chunk = largest_divisor(width, values.shape[1], 1024)
    vmem = pl.BlockSpec(memory_space=pltpu.VMEM)
    return pl.pallas_call(
        functools.partial(dense_kernel, lora_scale, grad_scale, tile, chunk),
        out_shape=(
            jax.ShapeDtypeStruct((rows, hidden), jnp.bfloat16),
            jax.ShapeDtypeStruct((parts, rows, width // parts), jnp.bfloat16),
            jax.ShapeDtypeStruct(values.shape, jnp.bfloat16),
        ),
        in_specs=[pl.BlockSpec(memory_space=pltpu.SMEM)]
        + [vmem] * 5
        + [pl.BlockSpec(memory_space=pl.ANY)],
        out_specs=(vmem, vmem, vmem),
        scratch_shapes=[
            pltpu.VMEM((2, tile, width), jnp.bfloat16),
            pltpu.VMEM((rows, tile), jnp.float32),
            pltpu.VMEM((rows, width), jnp.float32),
            pltpu.SemaphoreType.DMA((2,)),
        ],
        compiler_params=pltpu.CompilerParams(vmem_limit_bytes=60 * 1024 * 1024),
        cost_estimate=pl.CostEstimate(
            flops=4 * rows * hidden * width,
            bytes_accessed=2 * hidden * width + 4 * rows * width,
            transcendentals=0,
        ),
    )(ids, gathered, cotangent, hidden_half, u_half, values, base)


def shards(
    tokens, base_weight, block_values, block_ids, lowrank_model, lowrank_hidden, output_cotangent
):
    mp_size = lax.axis_size("mp")
    total_tokens = tokens.shape[0] * lax.axis_size("dp")
    feature_width = base_weight.shape[1]
    hidden_total = base_weight.shape[0] * mp_size
    rank = lowrank_model.shape[1]
    lora_scale = 0.5 / math.sqrt(rank * feature_width)

    model_half = lowrank_model.astype(jnp.bfloat16)
    hidden_half = lowrank_hidden.astype(jnp.bfloat16)
    gathered = lax.all_gather(tokens, "mp", axis=1, tiled=True)
    u_part = jnp.dot(tokens, model_half, preferred_element_type=jnp.float32)
    v_part = jnp.dot(output_cotangent, hidden_half, preferred_element_type=jnp.float32)
    both = lax.psum(jnp.stack([u_part, v_part]), "mp").astype(jnp.bfloat16)
    u_half, v_half = both[0], both[1]

    hidden_part = lora_scale * lax.dot_general(
        output_cotangent, u_half, (((0,), (0,)), ((), ())), preferred_element_type=jnp.float32
    )
    model_part = lora_scale * lax.dot_general(
        tokens, v_half, (((0,), (0,)), ((), ())), preferred_element_type=jnp.float32
    )
    grad_hidden, grad_model = lax.psum(
        (hidden_part.astype(jnp.bfloat16), model_part.astype(jnp.bfloat16)), "dp"
    )

    projection_output, back_parts, block_parts = dense(
        block_ids,
        gathered,
        output_cotangent,
        hidden_half,
        u_half,
        block_values,
        base_weight,
        mp_size,
        lora_scale,
        1.0 / math.sqrt(total_tokens),
    )

    model_step = lowrank_model - math.sqrt(
        rank * feature_width / (total_tokens * hidden_total)
    ) * grad_model.astype(jnp.float32)
    moved = lowrank_hidden - math.sqrt(rank / total_tokens) * grad_hidden.astype(jnp.float32)
    gram = lax.psum(
        lax.dot_general(moved, moved, (((0,), (0,)), ((), ())), precision=HIGHEST), "mp"
    )
    lower = lax.linalg.cholesky(gram, symmetrize_input=False)
    inverse = lax.linalg.triangular_solve(
        lower, math.sqrt(hidden_total) * jnp.eye(rank, dtype=jnp.float32), left_side=True, lower=True
    )
    updated_hidden = lax.dot_general(
        moved, inverse, (((1,), (1,)), ((), ())), precision=HIGHEST
    )
    updated_model = jnp.dot(model_step, lower, precision=HIGHEST) / math.sqrt(hidden_total)

    back = lax.psum_scatter(back_parts, "mp", scatter_dimension=0, tiled=False)
    lowrank_back = lax.dot_general(
        v_half, model_half, (((1,), (1,)), ((), ())), preferred_element_type=jnp.float32
    )
    input_cotangent = (back.astype(jnp.float32) + lora_scale * lowrank_back).astype(jnp.bfloat16)
    block_grads = lax.psum_scatter(block_parts, "dp", scatter_dimension=0, tiled=True).astype(
        jnp.float32
    )
    return (projection_output, input_cotangent, block_grads, updated_model, updated_hidden)


def solution(mesh):
    in_specs = (
        P("dp", "mp"),
        P("mp", None),
        P("mp", None, None),
        P(None, "mp"),
        P("mp", None),
        P("mp", None),
        P("dp", "mp"),
    )
    out_specs = (
        P("dp", "mp"),
        P("dp", "mp"),
        P(("mp", "dp"), None, None),
        P("mp", None),
        P("mp", None),
    )
    return jax.shard_map(shards, mesh=mesh, in_specs=in_specs, out_specs=out_specs, check_vma=False)
```

time: 541 us -> 284 us (0.52)
  matrix products: 231 us -> 28.8 us
  other arithmetic: 169 us -> 61.5 us
  Pallas kernels: 0 us -> 58.1 us
  waiting for transfers between devices: 31 us -> 65.3 us
  local copies, waits for them, and re-layouts: 41.3 us -> 14.5 us
    dot_general x17 -> x7, matrix products: 213 us -> 22.5 us  [the longest x1 6.77 us: shards(): lax.dot_general(moved, inverse, (((1,), (1,)), ((), ())), precision=HIGHEST)]
    another operation x30 -> x10, other arithmetic: 160 us -> 56.8 us  [the longest x6 34.6 us: shards(): lower = lax.linalg.cholesky(gram, symmetrize_input=False)]
    psum x1 -> x2, waiting for transfers between devices: 0.02 us -> 64.2 us  [the longest x1 64.2 us: shards(): lax.psum((hidden_part.astype(jnp.bfloat16), model_part.astype(jnp.bfloat1...]
    pallas_call x0 -> x1, Pallas kernels: none -> 58.1 us  [dense(): pl.pallas_call(functools.partial(dense_kernel, lora_scale, grad_scale, ti...]
    all_gather x1 -> x0, waiting for transfers between devices: 19.2 us -> none  [shards(): model_rows = lax.all_gather(model_half, 'mp', axis=0, tiled=True)]
    ppermute x3 -> x0, waiting for transfers between devices: 11.7 us -> none  [partner_2(): lax.ppermute(value, axis, [(i, i ^ 1 << distance) for i in range(lax.axis...]
    another operation x11 -> x5, matrix products: 15.3 us -> 5.64 us  [the longest x3 2.85 us: shards(): lax.linalg.triangular_solve(lower, math.sqrt(hidden_total) * jnp.eye(rank...]
    reshape x2 -> x0, local copies, waits for them, and re-layouts: 9.35 us -> none  [the longest x1 6.77 us: shards(): gathered.reshape(tok_rows, col_blocks, block_size)]
  transfers between devices with their start and end apart: 8 -> 5, of which waited for: 4 -> 1; matrix products, arithmetic and copies ran while one was open for 80% -> 34% of each run, Pallas kernels for 0% -> 21%
where the time goes in v1:
time: 284 us; the launch traced here: 282 us
  waiting for transfers between devices  65.3 us (23%)
  other arithmetic  61.5 us (22%)
  Pallas kernels  58.1 us (20%)
  blocking collectives  37 us (13%)
  matrix products  28.8 us (10%)
  between operations  16.6 us (6%)
  local copies, waits for them, and re-layouts  14.5 us (5%)
    psum x1, waiting for transfers between devices, shards(): lax.psum((hidden_part.astype(jnp.bfloat16), model_part.astype(jnp.bfloat1...  64.2 us
    pallas_call x1, Pallas kernels, dense(): pl.pallas_call(functools.partial(dense_kernel, lora_scale, grad_scale, ti...  58.1 us
    psum x1, blocking collectives, shards(): both = lax.psum(jnp.stack([u_part, v_part]), 'mp').astype(jnp.bfloat16)  37 us
    another operation x6, other arithmetic, shards(): lower = lax.linalg.cholesky(gram, symmetrize_input=False)  34.6 us
    another operation x3, other arithmetic, shards(): lax.linalg.triangular_solve(lower, math.sqrt(hidden_total) * jnp.eye(rank...  22.2 us
    another operation x6, local copies, waits for them, and re-layouts  6.98 us
    dot_general x1, matrix products, shards(): lax.dot_general(moved, inverse, (((1,), (1,)), ((), ())), precision=HIGHEST)  6.77 us
    dot_general x1, matrix products, shards(): lax.dot_general(moved, moved, (((0,), (0,)), ((), ())), precision=HIGHEST)  5.89 us
  transfers between devices with their start and end apart: 5, of which 1 were waited for; matrix products, arithmetic and copies ran while one was open for 34% of the time, Pallas kernels for 21%

profile of v1, /device:TPU:0, one launch (start us, length us, event | category | flops | bytes accessed | tf_op | source)
XLA Modules:
  0.0 282.2 jit_solution(8589718562786611605)
XLA Ops:
  8.1 2.2 convert_element_type.40.hid_ref
  11.5 37.0 %all-reduce.9 = bf16[2,256,256]{2,1,0:T(8,128)(2,1)S(1)} all-reduce(f32[2,256,256]{2,1,0:T(8,128)S(1)} %pad_maximum_fusion), channel_id=1, replica_groups=mesh['dp'=4,'mp'=8] {'mp'}, use_global_device_ids=true, to_apply=%region_0.0 | all-reduce | flops 131072 | bytes 786432 | tf_op jit(solution)/shard_map/psum | solution.py:163
  48.6 1.1 fusion.9
  49.7 1.7 fusion.1
  52.1 2.4 copy.13
  54.5 0.7 slice_bitcast_fusion.1.u_ref
  55.1 64.2 %all-reduce.8.cloned.1.call-done = (bf16[1024,256]{0,1:T(8,128)(2,1)}, bf16[3072,256]{0,1:T(8,128)(2,1)}) async-done(((bf16[1024,256]{0,1:T(8,128)(2,1)}, bf16[3072,256]{0,1:T(8,128)(2,1)}), (bf16[1024,256]{0,1:T(8,128)(2,1)}, bf16[3072,256]{0,1:T(8,128)(2,1)})) %all-reduce.8.cloned.1.call-update) | async-done | bytes 2097168 | tf_op jit(solution)/shard_map/psum | solution.py:172
  119.3 5.9 %fusion.3 = f32[256,256]{1,0:T(8,128)} fusion(f32[3072,256]{0,1:T(8,128)S(1)} %copy.13, bf16[3072,256]{0,1:T(8,128)(2,1)} %get-tuple-element.28), kind=kOutput, calls=%fused_computation.7 | convolution fusion | flops 2418278400 | bytes 4980736 | tf_op jit(solution)/shard_map/dot_general | solution.py:194
  125.3 58.1 %shard_map.110 = (bf16[256,3072]{1,0:T(8,128)(2,1)}, bf16[8,256,1024]{2,1,0:T(8,128)(2,1)}, bf16[32,128,128]{2,1,0:T(8,128)(2,1)}) custom-call(s32[2,32]{1,0:T(2,128)} %ids_ref.1, bf16[256,8192]{1,0:T(8,128)(2,1)} %all-gather.2.cloned.1.call-done.tok_ref, bf16[256,3072]{1,0:T(8,128)(2,1)} %cot_ref.1, bf16[3072,256]{1,0:T(8,128)(2,1)} %copy-done.3, ...), custom_call_target="tpu_custom_call" | custom-call | flops 25769803776 | bytes 58720256 | tf_op jit(solution)/shard_map/pallas_call | solution.py:122
  184.2 2.5 copy.12
  186.7 0.7 fusion.20
  187.5 0.8 cholesky.118
  188.3 11.7 %cholesky.50 = f32[128,128]{1,0:T(8,128)S(1)} custom-call(f32[128,128]{1,0:T(8,128)S(1)} %cholesky.118), custom_call_target="Cholesky" | custom-call | tf_op jit(solution)/shard_map/cholesky | solution.py:196
  200.0 0.7 cholesky.113
  200.8 9.8 %custom-call.11 = f32[1,128,128]{1,2,0:T(8,128)S(1)} custom-call(f32[1,128,128]{2,1,0:T(8,128)S(1)} %get-tuple-element.34), custom_call_target="InvertDiagBlocksLowerTriangular" | custom-call | tf_op jit(solution)/shard_map/cholesky | solution.py:196
  210.6 1.7 constant_dynamic-update-slice_fusion.1
  212.3 1.1 convolution_subtract_fusion.1
  213.4 11.7 %cholesky.105 = f32[128,128]{1,0:T(8,128)S(1)} custom-call(f32[128,128]{1,0:T(8,128)S(1)} %convolution_subtract_fusion.1), custom_call_target="Cholesky" | custom-call | tf_op jit(solution)/shard_map/cholesky | solution.py:196
  225.1 0.6 select_reduce_fusion
  225.7 0.7 compare_reduce_fusion
  227.7 1.7 fusion.17
  229.4 7.0 %while.1 = (s32[]{:T(128)}, f32[256,256]{1,0:T(8,128)}, s32[2,2]{1,0:T(2,128)S(1)}, f32[2,128,128]{2,1,0:T(8,128)}, s32[]{:T(128)}) while((s32[]{:T(128)}, f32[256,256]{1,0:T(8,128)}, s32[2,2]{1,0:T(2,128)S(1)}, f32[2,128,128]{2,1,0:T(8,128)}, s32[]{:T(128)}) %tuple.27), condition=%wide.while_cond, body=%wide.while_body.sunk | while | flops 2 | bytes 132205 | solution.py:197
  229.4 0.6 fusion.48
  230.1 2.9 %bitcast_dynamic-update-slice_fusion.2 = f32[2,128,128]{2,1,0:T(8,128)} fusion(f32[2,128,128]{2,1,0:T(8,128)} %get-tuple-element.76, s32[]{:T(128)S(6)} %copy.23, f32[256,256]{1,0:T(8,128)} %get-tuple-element.79, s32[]{:T(128)} %bitcast.48, s32[]{:T(128)} %bitcast.49), kind=kLoop, calls=%fused_computation.clone.1 | loop fusion | bytes 132100 | tf_op jit(solution)/shard_map/triangular_solve
  233.6 2.8 %bitcast_dynamic-update-slice_fusion.2 = f32[2,128,128]{2,1,0:T(8,128)} fusion(f32[2,128,128]{2,1,0:T(8,128)} %get-tuple-element.76, s32[]{:T(128)S(6)} %copy.23, f32[256,256]{1,0:T(8,128)} %get-tuple-element.79, s32[]{:T(128)} %bitcast.48, s32[]{:T(128)} %bitcast.49), kind=kLoop, calls=%fused_computation.clone.1 | loop fusion | bytes 132100 | tf_op jit(solution)/shard_map/triangular_solve
  236.4 20.5 %custom-call.12 = f32[2,128,128]{1,2,0:T(8,128)S(1)} custom-call(f32[2,128,128]{2,1,0:T(8,128)} %get-tuple-element.18), custom_call_target="InvertDiagBlocksLowerTriangular" | custom-call | tf_op jit(solution)/shard_map/triangular_solve | solution.py:197
  256.9 1.3 fusion.21
  258.3 1.2 convolution_subtract_fusion
  259.8 4.2 %convolution_multiply_fusion.3 = f32[1024,256]{1,0:T(8,128)} fusion(f32[1024,256]{0,1:T(8,128)} %copy.12, bf16[1024,256]{0,1:T(8,128)(2,1)} %get-tuple-element.27, f32[256,256]{1,0:T(8,128)} %get-tuple-element.32, pred[]{:T(512)S(6)} %cholesky.110), kind=kOutput, calls=%fused_computation.13 | convolution fusion | flops 806551552 | bytes 2883585 | tf_op jit(solution)/shard_map/dot_general | solution.py:203
  264.0 6.8 %fusion.2 = f32[3072,256]{1,0:T(8,128)} fusion(f32[3072,256]{0,1:T(8,128)S(1)} %copy.13, bf16[3072,256]{0,1:T(8,128)(2,1)S(1)} %copy-done.2, f32[128,256]{1,0:T(8,128)S(1)} %fusion.27, f32[128,256]{1,0:T(8,128)S(1)} %fusion.21), kind=kOutput, calls=%fused_computation.6 | convolution fusion | flops 2418343936 | bytes 8126464 | tf_op jit(solution)/shard_map/dot_general | solution.py:200
  270.8 1.8 convert_element_type.46
  272.6 2.5 fusion.7
  (35 shorter events, 3.8 us)
Async XLA Ops:
  8.0 2.4 copy-start.1
  8.0 3.0 %copy-start.4 = (bf16[256,1024]{1,0:T(8,128)(2,1)S(1)}, bf16[256,1024]{1,0:T(8,128)(2,1)}, u32[]{:S(2)}) copy-start(bf16[256,1024]{1,0:T(8,128)(2,1)} %param.7) | copy-start | bytes 1572868
  8.0 3.0 %copy-start = (f32[1024,256]{1,0:T(8,128)S(1)}, f32[1024,256]{1,0:T(8,128)}, u32[]{:S(2)}) copy-start(f32[1024,256]{1,0:T(8,128)} %param.11) | copy-start | bytes 3145732
  8.0 111.3 %all-reduce.8.cloned.1.call-start = ((), (), s32[]{:S(2)}) async-start(), calls=%async_computation.6 | async-start | bytes 4194304 | tf_op jit(solution)/shard_map/psum | solution.py:172
  10.4 1.1 copy-start.3
  51.4 73.9 %all-gather.2.cloned.1.call-start = ((), (), s32[]{:S(2)}) async-start(), calls=%async_computation.2 | async-start | bytes 4718592 | tf_op jit(solution)/shard_map/all_gather | solution.py:160
  52.0 135.4 %all-reduce.6.cloned.1.call-start = ((), (), s32[]{:S(2)}) async-start(), calls=%async_computation.5 | async-start | bytes 524288 | tf_op jit(solution)/shard_map/psum | solution.py:193
  125.2 145.6 %reduce-scatter.5.cloned.1.call-start = ((), (), s32[]{:S(2)}) async-start(), calls=%async_computation.4 | async-start | bytes 1310720 | tf_op jit(solution)/shard_map/reduce_scatter | solution.py:210
  183.5 89.1 %reduce-scatter.3.cloned.1.call-start = ((), (), s32[]{:S(2)}) async-start(), calls=%async_computation.3 | async-start | bytes 4718592 | tf_op jit(solution)/shard_map/reduce_scatter | solution.py:205
  256.9 7.1 %copy-start.2 = (bf16[3072,256]{0,1:T(8,128)(2,1)S(1)}, bf16[3072,256]{0,1:T(8,128)(2,1)}, u32[]{:S(2)}) copy-start(bf16[3072,256]{0,1:T(8,128)(2,1)} %get-tuple-element.28) | copy-start | bytes 4718596
Sparse Core Ops, SparseCore 0:
  51.6 67.6 all-reduce.7
  183.6 30.7 reduce-scatter.4
  216.6 49.8 reduce-scatter.2
Sparse Core Ops, SparseCore 1:
  53.5 44.9 all-gather.1
  125.3 55.4 all-reduce.5

commit v2 on v1

--- a/solution.py
+++ b/solution.py
@@ -145,6 +145,27 @@
     )(ids, gathered, cotangent, hidden_half, u_half, values, base)
 
 
+def factor_and_inverse(gram):
+    half = gram.shape[0] // 2
+    eye = jnp.eye(half, dtype=gram.dtype)
+    zero = jnp.zeros((half, half), gram.dtype)
+
+    def corner(block):
+        low = lax.linalg.cholesky(block, symmetrize_input=False)
+        return low, lax.linalg.triangular_solve(low, eye, left_side=True, lower=True)
+
+    low1, inv1 = corner(gram[:half, :half])
+    cross = lax.dot_general(
+        gram[half:, :half], inv1, (((1,), (1,)), ((), ())), precision=HIGHEST
+    )
+    square = lax.dot_general(cross, cross, (((1,), (1,)), ((), ())), precision=HIGHEST)
+    low2, inv2 = corner(gram[half:, half:] - square)
+    below = -jnp.dot(inv2, jnp.dot(cross, inv1, precision=HIGHEST), precision=HIGHEST)
+    lower = jnp.block([[low1, zero], [cross, low2]])
+    inverse = jnp.block([[inv1, zero], [below, inv2]])
+    return lower, inverse
+
+
 def shards(
     tokens, base_weight, block_values, block_ids, lowrank_model, lowrank_hidden, output_cotangent
 ):
@@ -193,10 +214,8 @@
     gram = lax.psum(
         lax.dot_general(moved, moved, (((0,), (0,)), ((), ())), precision=HIGHEST), "mp"
     )
-    lower = lax.linalg.cholesky(gram, symmetrize_input=False)
-    inverse = lax.linalg.triangular_solve(
-        lower, math.sqrt(hidden_total) * jnp.eye(rank, dtype=jnp.float32), left_side=True, lower=True
-    )
+    lower, inverse = factor_and_inverse(gram)
+    inverse = math.sqrt(hidden_total) * inverse
     updated_hidden = lax.dot_general(
         moved, inverse, (((1,), (1,)), ((), ())), precision=HIGHEST
     )

time: 284 us -> 276 us (0.972)
  other arithmetic: 61.5 us -> 55.8 us
  local copies, waits for them, and re-layouts: 14.5 us -> 9 us
  waiting for transfers between devices: 65.3 us -> 69.7 us
    another operation x9 -> x1, local copies, waits for them, and re-layouts: 8.62 us -> 1.56 us  [corner(): lax.linalg.triangular_solve(low, eye, left_side=True, lower=True)]
    another operation x9 -> x10, other arithmetic: 56.7 us -> 51.8 us  [the longest x6 27.1 us: corner(): low = lax.linalg.cholesky(block, symmetrize_input=False)]
    reduce_scatter x1, waiting for transfers between devices: 0.01 us -> 4.46 us  [shards(): back = lax.psum_scatter(back_parts, 'mp', scatter_dimension=0, tiled=False)]
    dot_general x0 -> x4, matrix products: none -> 4.44 us  [the longest x1 1.75 us: factor_and_inverse(): lax.dot_general(cross, cross, (((1,), (1,)), ((), ())), precision=HIGHEST)]
    another operation x5 -> x2, matrix products: 5.64 us -> 2.02 us  [corner(): lax.linalg.triangular_solve(low, eye, left_side=True, lower=True)]
  transfers between devices with their start and end apart: 5 -> 5, of which waited for: 1 -> 2; matrix products, arithmetic and copies ran while one was open for 34% -> 31% of each run, Pallas kernels for 21% -> 21%
where the time goes in v2:
time: 276 us; the launch traced here: 275 us
  waiting for transfers between devices  69.7 us (25%)
  Pallas kernels  58.5 us (21%)
  other arithmetic  55.8 us (20%)
  blocking collectives  37 us (13%)
  matrix products  29.6 us (11%)
  between operations  15.3 us (6%)
  local copies, waits for them, and re-layouts  9 us (3%)
    psum x1, waiting for transfers between devices, shards(): lax.psum((hidden_part.astype(jnp.bfloat16), model_part.astype(jnp.bfloat1...  64.2 us
    pallas_call x1, Pallas kernels, dense(): pl.pallas_call(functools.partial(dense_kernel, lora_scale, grad_scale, ti...  58.5 us
    psum x1, blocking collectives, shards(): both = lax.psum(jnp.stack([u_part, v_part]), 'mp').astype(jnp.bfloat16)  37 us
    another operation x6, other arithmetic, corner(): low = lax.linalg.cholesky(block, symmetrize_input=False)  27.1 us
    another operation x4, other arithmetic, corner(): lax.linalg.triangular_solve(low, eye, left_side=True, lower=True)  24.7 us
    dot_general x1, matrix products, shards(): lax.dot_general(moved, inverse, (((1,), (1,)), ((), ())), precision=HIGHEST)  6.76 us
    dot_general x1, matrix products, shards(): lax.dot_general(moved, moved, (((0,), (0,)), ((), ())), precision=HIGHEST)  5.89 us
  transfers between devices with their start and end apart: 5, of which 2 were waited for; matrix products, arithmetic and copies ran while one was open for 31% of the time, Pallas kernels for 21%

profile of v2, /device:TPU:0, one launch (start us, length us, event | category | flops | bytes accessed | tf_op | source)
XLA Modules:
  0.0 275.4 jit_solution(2039605405483676978)
XLA Ops:
  8.1 2.2 convert_element_type.44.hid_ref
  10.4 0.6 convolution_bitcast_fusion
  11.5 37.0 %all-reduce.10 = bf16[2,256,256]{2,1,0:T(8,128)(2,1)S(1)} all-reduce(f32[2,256,256]{2,1,0:T(8,128)S(1)} %pad_maximum_fusion), channel_id=1, replica_groups=mesh['dp'=4,'mp'=8] {'mp'}, use_global_device_ids=true, to_apply=%region_0.0 | all-reduce | flops 131072 | bytes 786432 | tf_op jit(solution)/shard_map/psum | solution.py:184
  48.6 1.1 fusion.9
  49.7 1.7 fusion.1
  52.1 2.4 copy.13
  54.5 0.7 slice_bitcast_fusion.1.u_ref
  55.1 64.2 %all-reduce.9.cloned.1.call-done = (bf16[1024,256]{0,1:T(8,128)(2,1)}, bf16[3072,256]{0,1:T(8,128)(2,1)}) async-done(((bf16[1024,256]{0,1:T(8,128)(2,1)}, bf16[3072,256]{0,1:T(8,128)(2,1)}), (bf16[1024,256]{0,1:T(8,128)(2,1)}, bf16[3072,256]{0,1:T(8,128)(2,1)})) %all-reduce.9.cloned.1.call-update) | async-done | bytes 2097168 | tf_op jit(solution)/shard_map/psum | solution.py:193
  119.3 5.9 %fusion.3 = f32[256,256]{1,0:T(8,128)} fusion(f32[3072,256]{0,1:T(8,128)S(1)} %copy.13, bf16[3072,256]{0,1:T(8,128)(2,1)} %get-tuple-element.14), kind=kOutput, calls=%fused_computation.5 | convolution fusion | flops 2418278400 | bytes 4980736 | tf_op jit(solution)/shard_map/dot_general | solution.py:215
  125.3 58.5 %shard_map.110 = (bf16[256,3072]{1,0:T(8,128)(2,1)}, bf16[8,256,1024]{2,1,0:T(8,128)(2,1)}, bf16[32,128,128]{2,1,0:T(8,128)(2,1)}) custom-call(s32[2,32]{1,0:T(2,128)} %ids_ref.1, bf16[256,8192]{1,0:T(8,128)(2,1)} %all-gather.2.cloned.1.call-done.tok_ref, bf16[256,3072]{1,0:T(8,128)(2,1)} %cot_ref.1, bf16[3072,256]{1,0:T(8,128)(2,1)} %copy-done.3, ...), custom_call_target="tpu_custom_call" | custom-call | flops 25769803776 | bytes 58720256 | tf_op jit(solution)/shard_map/pallas_call | solution.py:122
  184.6 2.5 copy.12
  187.1 0.8 slice.26
  188.0 11.7 %custom-call.8 = f32[128,128]{1,0:T(8,128)S(1)} custom-call(f32[128,128]{1,0:T(8,128)S(1)} %slice.26), custom_call_target="Cholesky" | custom-call | tf_op jit(solution)/shard_map/cholesky/custom-call.1 | solution.py:154
  199.7 0.6 compare_reduce_fusion.1
  200.4 1.3 select_bitcast_fusion.1
  201.7 9.8 %custom-call.9 = f32[1,128,128]{1,2,0:T(8,128)S(1)} custom-call(f32[1,128,128]{2,1,0:T(8,128)S(1)} %get-tuple-element.17), custom_call_target="InvertDiagBlocksLowerTriangular" | custom-call | tf_op jit(solution)/shard_map/triangular_solve/custom-call.0 | solution.py:155
  211.8 1.1 fusion.35
  212.9 0.7 copy.14
  213.6 1.8 convolution_subtract_fusion
  215.3 13.2 %custom-call.10 = f32[128,128]{1,0:T(8,128)} custom-call(f32[128,128]{1,0:T(8,128)} %convolution_subtract_fusion), custom_call_target="Cholesky" | custom-call | tf_op jit(solution)/shard_map/cholesky/custom-call.1 | solution.py:154
  228.5 0.9 select_reduce_fusion
  229.4 0.7 compare_reduce_fusion
  230.1 2.1 select_bitcast_fusion
  232.2 11.5 %custom-call.11 = f32[1,128,128]{1,2,0:T(8,128)} custom-call(f32[1,128,128]{2,1,0:T(8,128)} %get-tuple-element.15), custom_call_target="InvertDiagBlocksLowerTriangular" | custom-call | tf_op jit(solution)/shard_map/triangular_solve/custom-call.0 | solution.py:155
  243.7 1.7 fusion.31
  245.4 1.6 copy.15
  247.3 1.3 convolution_negate_fusion
  248.6 4.2 %convolution_multiply_fusion.3 = f32[1024,256]{1,0:T(8,128)} fusion(f32[1024,256]{0,1:T(8,128)} %copy.12, bf16[1024,256]{0,1:T(8,128)(2,1)} %get-tuple-element.13, f32[128,128]{1,0:T(8,128)} %get-tuple-element.18, f32[128,128]{1,0:T(8,128)} %get-tuple-element.16, f32[128,128]{1,0:T(8,128)} %copy.14), kind=kOutput, calls=%fused_computation.11 | convolution fusion | flops 806617088 | bytes 2818048 | tf_op jit(solution)/shard_map/dot_general | solution.py:222
  252.8 6.8 %fusion.2 = f32[3072,256]{1,0:T(8,128)} fusion(f32[3072,256]{0,1:T(8,128)S(1)} %copy.13, bf16[3072,256]{0,1:T(8,128)(2,1)S(1)} %copy-done.2, f32[128,128]{1,0:T(8,128)S(1)} %fusion.33, f32[128,128]{1,0:T(8,128)S(1)} %copy-done.5, f32[128,128]{1,0:T(8,128)S(1)} %convolution_negate_fusion), kind=kOutput, calls=%fused_computation.4 | convolution fusion | flops 2418606080 | bytes 8060928 | tf_op jit(solution)/shard_map/dot_general | solution.py:219
  259.5 1.8 convert_element_type.50
  261.3 4.5 %reduce-scatter.3.cloned.1.call-done = bf16[1,256,1024]{2,1,0:T(8,128)(2,1)} async-done(((bf16[8,256,1024]{2,1,0:T(8,128)(2,1)}), bf16[1,256,1024]{2,1,0:T(8,128)(2,1)}) %reduce-scatter.3.cloned.1.call-update) | async-done | bytes 524304 | tf_op jit(solution)/shard_map/reduce_scatter | solution.py:224
  265.8 2.5 fusion.7
  (30 shorter events, 2.7 us)
Async XLA Ops:
  8.0 2.4 copy-start.1
  8.0 3.0 %copy-start.4 = (bf16[256,1024]{1,0:T(8,128)(2,1)S(1)}, bf16[256,1024]{1,0:T(8,128)(2,1)}, u32[]{:S(2)}) copy-start(bf16[256,1024]{1,0:T(8,128)(2,1)} %param.10) | copy-start | bytes 1572868
  8.0 3.0 %copy-start = (f32[1024,256]{1,0:T(8,128)S(1)}, f32[1024,256]{1,0:T(8,128)}, u32[]{:S(2)}) copy-start(f32[1024,256]{1,0:T(8,128)} %param.14) | copy-start | bytes 3145732
  8.0 111.3 %all-reduce.9.cloned.1.call-start = ((), (), s32[]{:S(2)}) async-start(), calls=%async_computation.6 | async-start | bytes 4194304 | tf_op jit(solution)/shard_map/psum | solution.py:193
  10.4 1.1 copy-start.3
  51.4 73.9 %all-gather.2.cloned.1.call-start = ((), (), s32[]{:S(2)}) async-start(), calls=%async_computation.2 | async-start | bytes 4718592 | tf_op jit(solution)/shard_map/all_gather | solution.py:181
  52.0 135.1 %all-reduce.7.cloned.1.call-start = ((), (), s32[]{:S(2)}) async-start(), calls=%async_computation.5 | async-start | bytes 524288 | tf_op jit(solution)/shard_map/psum | solution.py:214
  125.2 134.3 %reduce-scatter.5.cloned.1.call-start = ((), (), s32[]{:S(2)}) async-start(), calls=%async_computation.4 | async-start | bytes 1310720 | tf_op jit(solution)/shard_map/reduce_scatter | solution.py:229
  183.9 81.9 %reduce-scatter.3.cloned.1.call-start = ((), (), s32[]{:S(2)}) async-start(), calls=%async_computation.3 | async-start | bytes 4718592 | tf_op jit(solution)/shard_map/reduce_scatter | solution.py:224
  247.0 5.8 %copy-start.2 = (bf16[3072,256]{0,1:T(8,128)(2,1)S(1)}, bf16[3072,256]{0,1:T(8,128)(2,1)}, u32[]{:S(2)}) copy-start(bf16[3072,256]{0,1:T(8,128)(2,1)} %get-tuple-element.14) | copy-start | bytes 4718596
  247.0 5.8 %copy-start.5 = (f32[128,128]{1,0:T(8,128)S(1)}, f32[128,128]{1,0:T(8,128)}, u32[]{:S(2)}) copy-start(f32[128,128]{1,0:T(8,128)} %copy.15) | copy-start | bytes 196612
Sparse Core Ops, SparseCore 0:
  51.6 67.6 all-reduce.8
  184.0 29.4 reduce-scatter.4
  215.8 49.9 reduce-scatter.2
Sparse Core Ops, SparseCore 1:
  53.5 44.9 all-gather.1
  125.3 55.4 all-reduce.6
